TPU v7x, 128 devices: a whole 4x4x4 slice. The times are simulated.
128 devices in a mesh: gx: 8 (over x, y_hi), gy: 16 (over z, y_lo, core).
Axes of the slice: x: 4, y: 4 (y_hi: 2, y_lo: 2; y = y_hi * 2 + y_lo), z: 4, core: 2. Of those that a mesh axis runs over, the one named last changes fastest.
Arguments:
- features: bfloat16 [16, 256, 256, 128], P(None, 'gx', 'gy'), may hold values from -24 to 24
- w_first: bfloat16 [27, 16, 16], replicated, may hold values from -0.3125 to 0.3125
- w_second: bfloat16 [27, 16, 16], replicated, may hold values from -0.3125 to 0.3125
- w_lift: bfloat16 [512, 16], replicated, may hold values from -1.5 to 1.5
- w_coarse: bfloat16 [512, 27, 512], P('gy'), may hold values from -0.0546875 to 0.0546875
- w_decode: bfloat16 [16, 512], replicated, may hold values from -0.25 to 0.25
- w_joining: bfloat16 [16, 32], replicated, may hold values from -1 to 1
Outputs:
- joined: bfloat16 [16, 256, 256, 128], P(None, 'gx', 'gy')
All inputs are finite; a program needn't handle non-finite values.
Results may differ from a plain program's by a relative error of at most 0.0065.
Values may be sent and summed in bfloat16 or wider, within the bound.
No kernel may reach another device: no remote copies, remote signals or barrier semaphores. Data moves between devices by JAX's collectives and lax.ppermute only.
A program may use at most 192 MiB of HBM per device.

v0:
```python
import jax
import jax.numpy as jnp
from jax import lax
from jax.experimental import pallas as pl
from jax.experimental.pallas import tpu as pltpu
from jax.sharding import PartitionSpec as P

POOL = 16
F32 = jnp.float32
BF16 = jnp.bfloat16


def iota(shape, dim):
    return lax.broadcasted_iota(jnp.int32, shape, dim)


def dot(a, b):
    return jnp.dot(a, b, preferred_element_type=F32)


def vmem_call(kernel, out_shape, scratch=(), flops=0, nbytes=0, smem=0):
    single = not isinstance(out_shape, (list, tuple))

    def call(*args):
        return pl.pallas_call(
            kernel,
            out_shape=out_shape,
            in_specs=[pl.BlockSpec(memory_space=pltpu.VMEM) for _ in args],
            out_specs=(
                pl.BlockSpec(memory_space=pltpu.VMEM)
                if single
                else [pl.BlockSpec(memory_space=pltpu.VMEM) for _ in out_shape]
            ),
            scratch_shapes=list(scratch),
            cost_estimate=pl.CostEstimate(flops=flops, bytes_accessed=nbytes, transcendentals=0),
        )(*args)

    return call


def pack_kernel(feat, xlo, xhi, ylo, yhi):
    size_x = feat.shape[1]
    for j in range(2):
        xlo[j] = feat[:, j].reshape(256, 128)
        xhi[j] = feat[:, size_x - 2 + j].reshape(256, 128)
    row, col = iota((64, 256), 0), iota((64, 256), 1)
    want = ((row >> 1) & 15) * 16 + (row & 1) + 14 * (row >> 5)
    select = jnp.where(col == want, 1.0, 0.0).astype(BF16)

    def step(p, carry):
        x = 2 * p
        both = jnp.concatenate(
            [feat[:, x].reshape(256, 128), feat[:, x + 1].reshape(256, 128)], axis=1
        )
        rows = dot(select, both).astype(BF16)
        for h in range(2):
            ylo[x + h] = rows[0:32, h * 128 : h * 128 + 128]
            yhi[x + h] = rows[32:64, h * 128 : h * 128 + 128]
        return carry

    lax.fori_loop(0, size_x // 2, step, 0)


def band(w_ref, wc_ref, t_ref, halo_rows, halo_cols):
    rows, cols = 256 + halo_rows, 256 + halo_cols
    crow, ccol = iota((16, cols), 0), iota((16, cols), 1)
    j = ccol - 256
    if halo_cols == 64:
        halo_in = (j >> 1) & 15
    else:
        halo_in = j & 15
    spread = jnp.where(jnp.where(ccol < 256, ccol >> 4, halo_in) == crow, 1.0, 0.0).astype(BF16)
    wc_ref[...] = dot(w_ref[...], spread).astype(BF16)
    r, o = iota((rows, 16), 0), iota((rows, 16), 1)
    expand = jnp.where(jnp.where(r < 256, r >> 4, r & 15) == o, 1.0, 0.0).astype(BF16)
    r, c = iota((rows, cols), 0), iota((rows, cols), 1)
    y_out = jnp.where(r < 256, r & 15, jnp.where(r < 272, -1, 16))
    j = c - 256
    if halo_cols == 64:
        y_halo = jnp.where(j < 32, (j & 1) - 2, (j & 1) + 16)
    else:
        y_halo = jnp.where(j < 16, -1, 16)
    y_in = jnp.where(c < 256, c & 15, y_halo)
    delta = y_in - y_out
    for off_c in range(3):
        for off_a in range(3):
            total = jnp.zeros((rows, cols), F32)
            for off_b in range(3):
                k = 9 * off_a + 3 * off_b + off_c
                value = dot(expand, wc_ref[16 * k : 16 * k + 16, :])
                total = jnp.where(delta == off_b - 1, value, total)
            total = total.astype(BF16)
            at = off_c * rows
            t_ref[at : at + rows, 256 * off_a : 256 * off_a + 256] = total[:, :256]
            left = 768 + halo_cols * off_a
            t_ref[at : at + rows, left : left + halo_cols] = total[:, 256:]


def prep_kernel(w1, w2, t1, t2, wc1, wc2):
    band(w1, wc1, t1, 32, 64)
    band(w2, wc2, t2, 0, 32)


def shifted_sum(acc, rows, half):
    lanes = slice(half * 128, half * 128 + 128)
    lane = iota((rows, 128), 1)
    before = pltpu.roll(acc[0:rows, lanes], 1, 1)
    after = pltpu.roll(acc[2 * rows : 3 * rows, lanes], 127, 1)
    total = acc[rows : 2 * rows, lanes]
    total = total + jnp.where(lane > 0, before, 0.0)
    total = total + jnp.where(lane < 127, after, 0.0)
    return jnp.maximum(total, 0.0)


def conv_kernel(
    feat, xl, xr, hl, hr, cl, cr, masks, t1, t2, second, pooled, fe, fh, f1, f1h, psum
):
    size_x = feat.shape[1]
    m_xl, m_xr = masks[0:1, :], masks[1:2, :]
    m_yl, m_yr = masks[2:3, :], masks[3:4, :]

    def scaled(v, m):
        return (v.astype(F32) * m).astype(BF16)

    def fill(x, carry):
        fe[x + 2] = feat[:, x].reshape(256, 128)
        fh[x + 2, 0:32] = scaled(hl[x], m_yl)
        fh[x + 2, 32:64] = scaled(hr[x], m_yr)
        return carry

    lax.fori_loop(0, size_x, fill, 0)
    for j in range(2):
        fe[j] = scaled(xl[j], m_xl)
        fh[j, 0:32] = scaled(cl[0, j], m_xl * m_yl)
        fh[j, 32:64] = scaled(cl[1, j], m_xl * m_yr)
        fe[size_x + 2 + j] = scaled(xr[j], m_xr)
        fh[size_x + 2 + j, 0:32] = scaled(cr[0, j], m_xr * m_yl)
        fh[size_x + 2 + j, 32:64] = scaled(cr[1, j], m_xr * m_yr)

    halo_row = iota((32, 128), 0)
    m_rim = jnp.where(halo_row < 16, m_yl, m_yr)

    def window(planes, rims, at, rim):
        return jnp.concatenate(
            [
                planes[pl.ds(at, 3)].reshape(768, 128),
                rims[pl.ds(at, 3)].reshape(3 * rim, 128),
            ],
            axis=0,
        )

    def conv_one(p, carry):
        at = 2 * p
        rhs = jnp.concatenate([window(fe, fh, at, 64), window(fe, fh, at + 1, 64)], axis=1)
        acc = dot(t1[...], rhs)
        for h in range(2):
            value = shifted_sum(acc, 288, h)
            f1[at + h] = value[:256].astype(BF16)
            f1h[at + h] = (value[256:] * m_rim).astype(BF16)
        return carry

    lax.fori_loop(0, (size_x + 2) // 2, conv_one, 0)
    f1[0] = scaled(f1[0], m_xl)
    f1h[0] = scaled(f1h[0], m_xl)
    f1[size_x + 1] = scaled(f1[size_x + 1], m_xr)
    f1h[size_x + 1] = scaled(f1h[size_x + 1], m_xr)

    z, lane = iota((128, 128), 0), iota((128, 128), 1)
    gather = jnp.where((z >> 4) == (lane & 7), 1.0, 0.0).astype(F32)
    keep = (iota((16, 128), 1) >> 3) == iota((16, 128), 0)
    results = []
    for block in range(size_x // POOL):
        psum[...] = jnp.zeros((256, 128), F32)

        def conv_two(q, carry):
            at = block * POOL + 2 * q
            rhs = jnp.concatenate([window(f1, f1h, at, 32), window(f1, f1h, at + 1, 32)], axis=1)
            acc = dot(t2[...], rhs)
            values = []
            for h in range(2):
                value = shifted_sum(acc, 256, h).astype(BF16)
                second[at + h] = value
                values.append(value.astype(F32))
            psum[...] += values[0] + values[1]
            return carry

        lax.fori_loop(0, POOL // 2, conv_two, 0)
        summed = jnp.sum(psum[...].reshape(16, 16, 128), axis=1)
        cells = jnp.dot(
            summed, gather, preferred_element_type=F32, precision=lax.Precision.HIGHEST
        )
        row = jnp.sum(jnp.where(keep, cells, 0.0), axis=0, keepdims=True) * (1.0 / POOL**3)
        results.append(row)
    both = jnp.concatenate(results, axis=0)
    for d in range(16):
        pooled[d] = both


def split3(v):
    a = v.astype(BF16)
    v = v - a.astype(F32)
    b = v.astype(BF16)
    c = (v - b.astype(F32)).astype(BF16)
    return a, b, c


def swap_groups(rows):
    lane = iota((256, 128), 1)
    major, minor = iota((256, 128), 0) >> 4, iota((256, 128), 0) & 15
    spread = jnp.broadcast_to(rows[:, None, :], (16, 16, 128)).reshape(256, 128)
    spread = jnp.where((lane >> 3) == minor, spread, 0.0)
    l0, l1 = iota((128, 128), 0), iota((128, 128), 1)
    fold = jnp.where((l0 & 7) == (l1 & 7), 1.0, 0.0).astype(BF16)
    out = []
    for piece in split3(spread):
        moved = jnp.where((lane >> 3) == major, dot(piece, fold), 0.0)
        out.append(jnp.sum(moved.reshape(16, 16, 128), axis=0))
    return out


def coarse_kernel(own, gl, gr, masks, w_lift, w_coarse, w_dec, out):
    m_xl, m_xr = masks[0:1, :], masks[1:2, :]
    slabs = [gl[...] * m_xl, own[:, 0, :], own[:, 1, :], gr[...] * m_xr]
    columns = []
    for slab in slabs:
        pieces = [v.astype(BF16) for v in swap_groups(slab)]
        columns.append(jnp.concatenate(pieces, axis=0))
    stacked = jnp.concatenate(columns, axis=1)
    lift = w_lift[...]
    lift3 = jnp.concatenate([lift, lift, lift], axis=1)
    lifted = jnp.maximum(dot(lift3, stacked), 0.0).astype(BF16)
    count = w_dec.shape[1]
    partial = dot(w_coarse[...], lifted)
    lane = iota((count, 128), 1)
    y, z = lane >> 3, lane & 7
    for x in range(2):
        total = jnp.zeros((count, 128), F32)
        for k in range(27):
            a, b, c = k // 9, k // 3 % 3 - 1, k % 3 - 1
            piece = partial[k * count : (k + 1) * count, (x + a) * 128 : (x + a) * 128 + 128]
            step = 8 * b + c
            if step:
                piece = pltpu.roll(piece, (-step) % 128, 1)
            good = None
            if b:
                good = (y < 15) if b > 0 else (y > 0)
            if c:
                inside = (z < 7) if c > 0 else (z > 0)
                good = inside if good is None else good & inside
            total = total + (piece if good is None else jnp.where(good, piece, 0.0))
        coarse = jnp.maximum(total, 0.0).astype(BF16)
        part = dot(w_dec[...], coarse)
        pieces = swap_groups(part)
        out[:, x, :] = pieces[0] + pieces[1] + pieces[2]


def join_kernel(second, parts, w_join, out):
    size_x = second.shape[0]
    r, c = iota((256, 16), 0), iota((256, 16), 1)
    rows = jnp.where((r >> 4) == c, 1.0, 0.0).astype(BF16)
    mixed = dot(rows, w_join[...]).astype(BF16)
    skip = mixed[:, 0:16]
    up = mixed[:, 16:32]
    r, c = iota((16, 256), 0), iota((16, 256), 1)
    cols = jnp.where((c >> 4) == r, 1.0, 0.0).astype(BF16)
    r, c = iota((256, 256), 0), iota((256, 256), 1)
    matrix = jnp.where((r & 15) == (c & 15), dot(skip, cols), 0.0).astype(BF16)
    keep = (iota((16, 128), 1) >> 3) == iota((16, 128), 0)
    l0, l1 = iota((128, 128), 0), iota((128, 128), 1)
    widen = jnp.where((l0 & 7) == (l1 >> 4), 1.0, 0.0).astype(BF16)
    total = parts[0]
    for d in range(1, 16):
        total = total + parts[d]
    for block in range(size_x // POOL):
        decoded = jnp.broadcast_to(total[block : block + 1, :], (16, 128))
        decoded = jnp.where(keep, decoded, 0.0).astype(BF16)
        cells = dot(decoded, widen).astype(BF16)
        term = dot(up, cells)
        term = jnp.concatenate([term, term], axis=1)

        def step(q, carry):
            x = block * POOL + 2 * q
            both = jnp.concatenate([second[x], second[x + 1]], axis=1)
            value = (dot(matrix, both) + term).astype(BF16)
            for h in range(2):
                out[:, x + h] = value[:, h * 128 : h * 128 + 128].reshape(16, 16, 128)
            return carry

        lax.fori_loop(0, POOL // 2, step, 0)


def local(features, w_first, w_second, w_lift, w_coarse, w_decode, w_joining):
    size_x = features.shape[1]
    nx, ny = lax.axis_size("gx"), lax.axis_size("gy")
    gx, gy = lax.axis_index("gx"), lax.axis_index("gy")

    def ring(count, step):
        return [(i, (i + step) % count) for i in range(count)]

    def shape(*dims, dtype=BF16):
        return jax.ShapeDtypeStruct(dims, dtype)

    row = lax.broadcasted_iota(jnp.int32, (8, 128), 0)
    masks = jnp.where(
        row == 0, gx > 0, jnp.where(row == 1, gx < nx - 1, jnp.where(row == 2, gy > 0, gy < ny - 1))
    ).astype(F32)

    xlo, xhi, ylo, yhi = vmem_call(
        pack_kernel,
        [shape(2, 256, 128), shape(2, 256, 128), shape(size_x, 32, 128), shape(size_x, 32, 128)],
        flops=2 * 64 * 256 * 128 * size_x,
        nbytes=3 << 20,
    )(features)
    hl = lax.ppermute(yhi, "gy", ring(ny, 1))
    hr = lax.ppermute(ylo, "gy", ring(ny, -1))
    xl = lax.ppermute(xhi, "gx", ring(nx, 1))
    xr = lax.ppermute(xlo, "gx", ring(nx, -1))
    cl = lax.ppermute(jnp.stack([hl[size_x - 2 :], hr[size_x - 2 :]]), "gx", ring(nx, 1))
    cr = lax.ppermute(jnp.stack([hl[:2], hr[:2]]), "gx", ring(nx, -1))

    t1, t2 = vmem_call(
        prep_kernel,
        [shape(864, 960), shape(768, 864)],
        scratch=[pltpu.VMEM((432, 320), BF16), pltpu.VMEM((432, 288), BF16)],
        flops=2 * 27 * 288 * 256 * 320,
        nbytes=4 << 20,
    )(w_first.reshape(432, 16), w_second.reshape(432, 16))
    count = w_coarse.shape[0]
    w_rows = jnp.transpose(w_coarse, (1, 0, 2)).reshape(27 * count, w_coarse.shape[2])
    w_dec = lax.dynamic_slice_in_dim(w_decode, gy * count, count, axis=1)

    second, pooled = vmem_call(
        conv_kernel,
        [shape(size_x, 256, 128), shape(16, 2, 128, dtype=F32)],
        scratch=[
            pltpu.VMEM((size_x + 4, 256, 128), BF16),
            pltpu.VMEM((size_x + 4, 64, 128), BF16),
            pltpu.VMEM((size_x + 2, 256, 128), BF16),
            pltpu.VMEM((size_x + 2, 32, 128), BF16),
            pltpu.VMEM((256, 128), F32),
        ],
        flops=2 * 2 * 864 * 960 * 128 * size_x,
        nbytes=9 << 20,
    )(features, xl, xr, hl, hr, cl, cr, masks, t1, t2)

    gathered = lax.all_to_all(pooled, "gy", 0, 0)
    gl = lax.ppermute(gathered[:, 1, :], "gx", ring(nx, 1))
    gr = lax.ppermute(gathered[:, 0, :], "gx", ring(nx, -1))
    parts = vmem_call(
        coarse_kernel,
        shape(16, 2, 128, dtype=F32),
        flops=2 * 864 * 512 * 512,
        nbytes=2 << 20,
    )(gathered, gl, gr, masks, w_lift, w_rows, w_dec)
    parts = lax.all_to_all(parts, "gy", 0, 0)
    joined = vmem_call(
        join_kernel,
        shape(16, size_x, 16, 128),
        flops=2 * 256 * 256 * 128 * size_x,
        nbytes=4 << 20,
    )(second, parts, w_joining)
    return joined


def solution(mesh):
    in_specs = (P(None, "gx", "gy", None), P(), P(), P(), P("gy", None, None), P(), P())
    out_specs = P(None, "gx", "gy", None)
    return jax.shard_map(local, mesh=mesh, in_specs=in_specs, out_specs=out_specs, check_vma=False)
```

profile of v0, /device:TPU:1, one launch (start us, length us, event | category | flops | bytes accessed | tf_op | source)
XLA Modules:
  0.0 100.3 jit_solution(15745224513576682936)
XLA Ops:
  0.0 0.0 copy-start
  0.0 0.0 copy-start.2
  0.0 0.0 copy-start.3
  0.0 5.0 %shard_map.73 = (bf16[2,256,128]{2,1,0:T(8,128)(2,1)}, bf16[2,256,128]{2,1,0:T(8,128)(2,1)}, bf16[32,32,128]{2,1,0:T(8,128)(2,1)}, bf16[32,32,128]{2,1,0:T(8,128)(2,1)}) custom-call(bf16[16,32,16,128]{3,2,1,0:T(8,128)(2,1)} %feat.3), custom_call_target="tpu_custom_call" | custom-call | flops 134217728 | bytes 3145728 | tf_op jit(solution)/shard_map/pallas_call | solution.py:25
  5.0 2.7 %collective-permute-start.2 = (bf16[32,32,128]{2,1,0:T(8,128)(2,1)}, bf16[32,32,128]{2,1,0:T(8,128)(2,1)S(1)}, u32[]{:S(2)}, u32[]{:S(2)}) collective-permute-start(bf16[32,32,128]{2,1,0:T(8,128)(2,1)} %get-tuple-element.15), channel_id=1, source_target_pairs={{0,1},{1,2},{2,3},{3,4},{4,5},{5,6},{6,7},{7,8},{8,9},{9,10},{10,1... | collective-permute-start | bytes 786440 | tf_op jit(solution)/shard_map/ppermute | solution.py:314
  7.6 0.0 collective-permute-start.3
  7.6 2.6 %collective-permute-start = (bf16[2,256,128]{2,1,0:T(8,128)(2,1)}, bf16[2,256,128]{2,1,0:T(8,128)(2,1)S(1)}, u32[]{:S(2)}, u32[]{:S(2)}) collective-permute-start(bf16[2,256,128]{2,1,0:T(8,128)(2,1)} %get-tuple-element.13), channel_id=1, source_target_pairs={{0,16},{16,32},{32,48},{48,64},{64,80},{80,96},{96,112},{112,0},{1... | collective-permute-start | bytes 393224 | tf_op jit(solution)/shard_map/ppermute | solution.py:316
  10.3 2.5 %collective-permute-start.1 = (bf16[2,256,128]{2,1,0:T(8,128)(2,1)}, bf16[2,256,128]{2,1,0:T(8,128)(2,1)S(1)}, u32[]{:S(2)}, u32[]{:S(2)}) collective-permute-start(bf16[2,256,128]{2,1,0:T(8,128)(2,1)} %get-tuple-element.14), channel_id=1, source_target_pairs={{0,112},{16,0},{32,16},{48,32},{64,48},{80,64},{96,80},{112,96},{1... | collective-permute-start | bytes 393224 | tf_op jit(solution)/shard_map/ppermute | solution.py:317
  12.7 0.0 copy-done.2
  12.7 0.8 copy.13
  13.6 0.0 copy-done.3
  13.6 0.8 copy.14
  14.4 5.5 %shard_map.74 = (bf16[864,960]{1,0:T(8,128)(2,1)}, bf16[768,864]{1,0:T(8,128)(2,1)}) custom-call(bf16[432,16]{1,0:T(8,128)(2,1)} %bitcast.19, bf16[432,16]{1,0:T(8,128)(2,1)} %bitcast.20), custom_call_target="tpu_custom_call" | custom-call | flops 1274019840 | bytes 4194304 | tf_op jit(solution)/shard_map/pallas_call | solution.py:25
  19.9 0.0 collective-permute-done.2.hl
  19.9 0.0 copy-start.5
  19.9 0.0 collective-permute-done.3.hr
  19.9 0.0 copy-start.6
  19.9 4.5 %collective-permute-start.5 = (bf16[2,2,32,128]{3,2,1,0:T(8,128)(2,1)S(1)}, bf16[2,2,32,128]{3,2,1,0:T(8,128)(2,1)S(1)}, u32[]{:S(2)}, u32[]{:S(2)}) collective-permute-start(bf16[2,2,32,128]{3,2,1,0:T(8,128)(2,1)S(1)} %pad_maximum_fusion.1), channel_id=1, source_target_pairs={{0,112},{16,0},{32,16},{48,32},{64,48},{80,64},{96,80},{112,96},{1... | collective-permute-start | bytes 98312 | tf_op jit(solution)/shard_map/ppermute | solution.py:319
  24.5 0.0 collective-permute-start.4
  24.5 0.0 collective-permute-done.xl
  24.5 0.0 copy-start.7
  24.5 0.0 collective-permute-done.1.xr
  24.5 0.0 copy-start.8
  24.5 1.0 collective-permute-done.5.cr
  25.5 0.0 copy-start.9
  25.5 5.4 %collective-permute-done.4.cl = bf16[2,2,32,128]{3,2,1,0:T(8,128)(2,1)S(1)} collective-permute-done((bf16[2,2,32,128]{3,2,1,0:T(8,128)(2,1)S(1)}, bf16[2,2,32,128]{3,2,1,0:T(8,128)(2,1)S(1)}, u32[]{:S(2)}, u32[]{:S(2)}) %collective-permute-start.4) | collective-permute-done | bytes 32800 | tf_op jit(solution)/shard_map/ppermute | solution.py:318
  30.8 0.0 copy-start.10
  30.8 0.7 iota.13.masks
  31.5 0.0 copy-done.5
  31.5 0.0 copy-done.6
  31.5 0.0 copy-done.7
  31.5 0.0 copy-done.8
  31.5 0.0 copy-done.9
  31.5 0.0 copy-done.10
  31.5 0.0 copy-start.4
  31.5 27.2 %shard_map.75 = (bf16[32,256,128]{2,1,0:T(8,128)(2,1)}, f32[16,2,128]{2,1,0:T(2,128)}) custom-call(bf16[16,32,16,128]{3,2,1,0:T(8,128)(2,1)} %feat.3, bf16[2,256,128]{2,1,0:T(8,128)(2,1)} %copy-done.7, bf16[2,256,128]{2,1,0:T(8,128)(2,1)} %copy-done.8, bf16[32,32,128]{2,1,0:T(8,128)(2,1)} %copy-done.5, bf16[32,32,128]{2,1,0:T(8,128)(2,1)} %copy-done.6, ...), custom_call_target="tpu_custom_call" | custom-call | flops 13589544960 | bytes 9437184 | tf_op jit(solution)/shard_map/pallas_call | solution.py:25
  58.8 7.3 %all-to-all-start = ((f32[16,2,128]{2,1,0:T(2,128)}), f32[16,2,128]{2,1,0:T(2,128)S(1)}, u32[]{:S(2)}, u32[]{:S(2)}) async-start(f32[16,2,128]{2,1,0:T(2,128)} %get-tuple-element.20), calls=%async_computation | async-start | bytes 32768 | tf_op jit(solution)/shard_map/all_to_all | solution.py:346
  66.1 5.8 %all-to-all-done.own = f32[16,2,128]{2,1,0:T(2,128)S(1)} async-done(((f32[16,2,128]{2,1,0:T(2,128)}), f32[16,2,128]{2,1,0:T(2,128)S(1)}, u32[]{:S(2)}, u32[]{:S(2)}) %all-to-all-start) | async-done | bytes 16416 | tf_op jit(solution)/shard_map/all_to_all | solution.py:346
  71.9 0.0 copy-start.1
  71.9 0.1 collective-permute-start.6
  72.0 5.1 %collective-permute-start.7 = (f32[16,128]{1,0:T(8,128)S(1)}, f32[16,128]{1,0:T(8,128)S(1)}, u32[]{:S(2)}, u32[]{:S(2)}) collective-permute-start(f32[16,128]{1,0:T(8,128)S(1)} %bitcast.21), channel_id=1, source_target_pairs={{0,112},{16,0},{32,16},{48,32},{64,48},{80,64},{96,80},{112,96},{1... | collective-permute-start | bytes 24584 | tf_op jit(solution)/shard_map/ppermute | solution.py:348
  77.0 0.0 copy-done
  77.0 0.7 constant_dynamic-slice_fusion.w_dec
  77.7 0.0 copy-done.4
  77.7 0.8 copy.17.w_lift
  78.5 0.0 collective-permute-done.6.gl
  78.5 0.0 copy-start.11
  78.5 0.0 collective-permute-done.7.gr
  78.5 0.0 copy-start.12
  78.5 0.0 copy-done.1
  78.5 0.6 copy-done.11
  79.1 0.0 copy-done.12
  79.1 3.6 %shard_map.76 = f32[16,2,128]{2,1,0:T(2,128)} custom-call(f32[16,2,128]{2,1,0:T(2,128)} %copy-done.1, f32[16,128]{1,0:T(8,128)} %copy-done.11, f32[16,128]{1,0:T(8,128)} %copy-done.12, f32[8,128]{1,0:T(8,128)} %iota.13.masks, bf16[512,16]{1,0:T(8,128)(2,1)} %copy.17.w_lift, bf16[864,512]{1,0:T(8,128)(2,1)} %bitcast.23, ...), custom_call_target="tpu_custom_call" | custom-call | flops 452984832 | bytes 2097152 | tf_op jit(solution)/shard_map/pallas_call | solution.py:25
  82.7 10.9 %all_to_all.10.parts = f32[16,2,128]{2,1,0:T(2,128)} all-to-all(f32[16,2,128]{2,1,0:T(2,128)} %shard_map.76), channel_id=1, replica_groups=mesh['gx'=8,'gy'=16] {'gy'}, dimensions={0} | all-to-all | bytes 32768 | tf_op jit(solution)/shard_map/all_to_all | solution.py:355
  93.6 6.7 %shard_map.77 = bf16[16,32,16,128]{3,2,1,0:T(8,128)(2,1)} custom-call(bf16[32,256,128]{2,1,0:T(8,128)(2,1)} %get-tuple-element.19.second, f32[16,2,128]{2,1,0:T(2,128)} %all_to_all.10.parts, bf16[16,32]{1,0:T(8,128)(2,1)} %w_join.1), custom_call_target="tpu_custom_call" | custom-call | flops 536870912 | bytes 4194304 | tf_op jit(solution)/shard_map/pallas_call | solution.py:25
  (6 shorter events, 0.0 us)
Async XLA Ops:
  0.0 77.0 %copy-start = (bf16[16,512]{1,0:T(8,128)(2,1)S(1)}, bf16[16,512]{1,0:T(8,128)(2,1)}, u32[]{:S(2)}) copy-start(bf16[16,512]{1,0:T(8,128)(2,1)} %param.12) | copy-start | bytes 49156
  0.0 12.7 %copy-start.2 = (bf16[27,16,16]{0,2,1:T(8,128)(2,1)S(1)}, bf16[27,16,16]{0,2,1:T(8,128)(2,1)}, u32[]{:S(2)}) copy-start(bf16[27,16,16]{0,2,1:T(8,128)(2,1)} %param.8) | copy-start | bytes 41476
  0.0 13.6 %copy-start.3 = (bf16[27,16,16]{0,2,1:T(8,128)(2,1)S(1)}, bf16[27,16,16]{0,2,1:T(8,128)(2,1)}, u32[]{:S(2)}) copy-start(bf16[27,16,16]{0,2,1:T(8,128)(2,1)} %param.9) | copy-start | bytes 41476
  5.0 14.9 %collective-permute-start.2 = (bf16[32,32,128]{2,1,0:T(8,128)(2,1)}, bf16[32,32,128]{2,1,0:T(8,128)(2,1)S(1)}, u32[]{:S(2)}, u32[]{:S(2)}) collective-permute-start(bf16[32,32,128]{2,1,0:T(8,128)(2,1)} %get-tuple-element.15), channel_id=1, source_target_pairs={{0,1},{1,2},{2,3},{3,4},{4,5},{5,6},{6,7},{7,8},{8,9},{9,10},{10,1... | collective-permute-start | bytes 786440 | tf_op jit(solution)/shard_map/ppermute | solution.py:314
  7.6 12.3 %collective-permute-start.3 = (bf16[32,32,128]{2,1,0:T(8,128)(2,1)}, bf16[32,32,128]{2,1,0:T(8,128)(2,1)S(1)}, u32[]{:S(2)}, u32[]{:S(2)}) collective-permute-start(bf16[32,32,128]{2,1,0:T(8,128)(2,1)} %get-tuple-element.16), channel_id=1, source_target_pairs={{0,15},{1,0},{2,1},{3,2},{4,3},{5,4},{6,5},{7,6},{8,7},{9,8},{10,9... | collective-permute-start | bytes 786440 | tf_op jit(solution)/shard_map/ppermute | solution.py:315
  7.6 16.8 %collective-permute-start = (bf16[2,256,128]{2,1,0:T(8,128)(2,1)}, bf16[2,256,128]{2,1,0:T(8,128)(2,1)S(1)}, u32[]{:S(2)}, u32[]{:S(2)}) collective-permute-start(bf16[2,256,128]{2,1,0:T(8,128)(2,1)} %get-tuple-element.13), channel_id=1, source_target_pairs={{0,16},{16,32},{32,48},{48,64},{64,80},{80,96},{96,112},{112,0},{1... | collective-permute-start | bytes 393224 | tf_op jit(solution)/shard_map/ppermute | solution.py:316
  10.3 14.2 %collective-permute-start.1 = (bf16[2,256,128]{2,1,0:T(8,128)(2,1)}, bf16[2,256,128]{2,1,0:T(8,128)(2,1)S(1)}, u32[]{:S(2)}, u32[]{:S(2)}) collective-permute-start(bf16[2,256,128]{2,1,0:T(8,128)(2,1)} %get-tuple-element.14), channel_id=1, source_target_pairs={{0,112},{16,0},{32,16},{48,32},{64,48},{80,64},{96,80},{112,96},{1... | collective-permute-start | bytes 393224 | tf_op jit(solution)/shard_map/ppermute | solution.py:317
  19.9 11.6 %copy-start.5 = (bf16[32,32,128]{2,1,0:T(8,128)(2,1)}, bf16[32,32,128]{2,1,0:T(8,128)(2,1)S(1)}, u32[]{:S(2)}) copy-start(bf16[32,32,128]{2,1,0:T(8,128)(2,1)S(1)} %collective-permute-done.2.hl) | copy-start | bytes 786436
  19.9 11.6 %copy-start.6 = (bf16[32,32,128]{2,1,0:T(8,128)(2,1)}, bf16[32,32,128]{2,1,0:T(8,128)(2,1)S(1)}, u32[]{:S(2)}) copy-start(bf16[32,32,128]{2,1,0:T(8,128)(2,1)S(1)} %collective-permute-done.3.hr) | copy-start | bytes 786436
  19.9 5.5 %collective-permute-start.5 = (bf16[2,2,32,128]{3,2,1,0:T(8,128)(2,1)S(1)}, bf16[2,2,32,128]{3,2,1,0:T(8,128)(2,1)S(1)}, u32[]{:S(2)}, u32[]{:S(2)}) collective-permute-start(bf16[2,2,32,128]{3,2,1,0:T(8,128)(2,1)S(1)} %pad_maximum_fusion.1), channel_id=1, source_target_pairs={{0,112},{16,0},{32,16},{48,32},{64,48},{80,64},{96,80},{112,96},{1... | collective-permute-start | bytes 98312 | tf_op jit(solution)/shard_map/ppermute | solution.py:319
  24.5 6.4 %collective-permute-start.4 = (bf16[2,2,32,128]{3,2,1,0:T(8,128)(2,1)S(1)}, bf16[2,2,32,128]{3,2,1,0:T(8,128)(2,1)S(1)}, u32[]{:S(2)}, u32[]{:S(2)}) collective-permute-start(bf16[2,2,32,128]{3,2,1,0:T(8,128)(2,1)S(1)} %pad_maximum_fusion), channel_id=1, source_target_pairs={{0,16},{16,32},{32,48},{48,64},{64,80},{80,96},{96,112},{112,0},{1... | collective-permute-start | bytes 98312 | tf_op jit(solution)/shard_map/ppermute | solution.py:318
  24.5 7.0 %copy-start.7 = (bf16[2,256,128]{2,1,0:T(8,128)(2,1)}, bf16[2,256,128]{2,1,0:T(8,128)(2,1)S(1)}, u32[]{:S(2)}) copy-start(bf16[2,256,128]{2,1,0:T(8,128)(2,1)S(1)} %collective-permute-done.xl) | copy-start | bytes 393220
  24.5 7.0 %copy-start.8 = (bf16[2,256,128]{2,1,0:T(8,128)(2,1)}, bf16[2,256,128]{2,1,0:T(8,128)(2,1)S(1)}, u32[]{:S(2)}) copy-start(bf16[2,256,128]{2,1,0:T(8,128)(2,1)S(1)} %collective-permute-done.1.xr) | copy-start | bytes 393220
  25.5 6.0 %copy-start.9 = (bf16[2,2,32,128]{3,2,1,0:T(8,128)(2,1)}, bf16[2,2,32,128]{3,2,1,0:T(8,128)(2,1)S(1)}, u32[]{:S(2)}) copy-start(bf16[2,2,32,128]{3,2,1,0:T(8,128)(2,1)S(1)} %collective-permute-done.5.cr) | copy-start | bytes 98308
  30.8 0.7 copy-start.10
  31.5 46.2 %copy-start.4 = (bf16[512,16]{0,1:T(8,128)(2,1)S(1)}, bf16[512,16]{0,1:T(8,128)(2,1)}, u32[]{:S(2)}) copy-start(bf16[512,16]{0,1:T(8,128)(2,1)} %param.10) | copy-start | bytes 49156
  58.8 13.1 %all-to-all-start = ((f32[16,2,128]{2,1,0:T(2,128)}), f32[16,2,128]{2,1,0:T(2,128)S(1)}, u32[]{:S(2)}, u32[]{:S(2)}) async-start(f32[16,2,128]{2,1,0:T(2,128)} %get-tuple-element.20), calls=%async_computation | async-start | bytes 32768 | tf_op jit(solution)/shard_map/all_to_all | solution.py:346
  71.9 6.6 %copy-start.1 = (f32[16,2,128]{2,1,0:T(2,128)}, f32[16,2,128]{2,1,0:T(2,128)S(1)}, u32[]{:S(2)}) copy-start(f32[16,2,128]{2,1,0:T(2,128)S(1)} %all-to-all-done.own) | copy-start | bytes 49156
  71.9 6.6 %collective-permute-start.6 = (f32[16,128]{1,0:T(8,128)S(1)}, f32[16,128]{1,0:T(8,128)S(1)}, u32[]{:S(2)}, u32[]{:S(2)}) collective-permute-start(f32[16,128]{1,0:T(8,128)S(1)} %bitcast.22), channel_id=1, source_target_pairs={{0,16},{16,32},{32,48},{48,64},{64,80},{80,96},{96,112},{112,0},{1... | collective-permute-start | bytes 24584 | tf_op jit(solution)/shard_map/ppermute | solution.py:347
  72.0 6.5 %collective-permute-start.7 = (f32[16,128]{1,0:T(8,128)S(1)}, f32[16,128]{1,0:T(8,128)S(1)}, u32[]{:S(2)}, u32[]{:S(2)}) collective-permute-start(f32[16,128]{1,0:T(8,128)S(1)} %bitcast.21), channel_id=1, source_target_pairs={{0,112},{16,0},{32,16},{48,32},{64,48},{80,64},{96,80},{112,96},{1... | collective-permute-start | bytes 24584 | tf_op jit(solution)/shard_map/ppermute | solution.py:348
  78.5 0.6 copy-start.11
  78.5 0.6 copy-start.12
where the time goes:
time: 101 us; the launch traced here: 100 us
  Pallas kernels  47.9 us (47%)
  starting transfers between devices  24.7 us (24%)
  waiting for transfers between devices  12.1 us (12%)
  blocking collectives  10.9 us (11%)
  local copies, waits for them, and re-layouts  4.4 us (4%)
    pallas_call x5, Pallas kernels, call(): pl.pallas_call(kernel, out_shape=out_shape, in_specs=[pl.BlockSpec(memory...  47.9 us
    all_to_all x1, blocking collectives, local(): parts = lax.all_to_all(parts, 'gy', 0, 0)  10.9 us
    all_to_all x1, starting transfers between devices, local(): gathered = lax.all_to_all(pooled, 'gy', 0, 0)  7.32 us
    all_to_all x1, waiting for transfers between devices, local(): gathered = lax.all_to_all(pooled, 'gy', 0, 0)  5.79 us
    ppermute x1, waiting for transfers between devices, local(): lax.ppermute(jnp.stack([hl[size_x - 2:], hr[size_x - 2:]]), 'gx', ring(nx...  5.36 us
    ppermute x1, starting transfers between devices, local(): gr = lax.ppermute(gathered[:, 0, :], 'gx', ring(nx, -1))  5.07 us
    ppermute x1, starting transfers between devices, local(): cr = lax.ppermute(jnp.stack([hl[:2], hr[:2]]), 'gx', ring(nx, -1))  4.52 us
    unnamed x29, local copies, waits for them, and re-layouts  3.05 us
  transfers between devices with their start and end apart: 9, of which 3 were waited for; matrix products, arithmetic and copies ran while one was open for 3% of the time, Pallas kernels for 5%

commit v1 on v0

v1 whole, which is shorter than its diff:
```python
import jax
import jax.numpy as jnp
from jax import lax
from jax.experimental import pallas as pl
from jax.experimental.pallas import tpu as pltpu
from jax.sharding import PartitionSpec as P

POOL = 16
F32 = jnp.float32
BF16 = jnp.bfloat16


def iota(shape, dim):
    return lax.broadcasted_iota(jnp.int32, shape, dim)


def dot(a, b):
    return jnp.dot(a, b, preferred_element_type=F32)


def vmem_call(kernel, out_shape, scratch=(), flops=0, nbytes=0, smem=0):
    single = not isinstance(out_shape, (list, tuple))

    def call(*args):
        return pl.pallas_call(
            kernel,
            out_shape=out_shape,
            in_specs=[pl.BlockSpec(memory_space=pltpu.VMEM) for _ in args],
            out_specs=(
                pl.BlockSpec(memory_space=pltpu.VMEM)
                if single
                else [pl.BlockSpec(memory_space=pltpu.VMEM) for _ in out_shape]
            ),
            scratch_shapes=list(scratch),
            cost_estimate=pl.CostEstimate(flops=flops, bytes_accessed=nbytes, transcendentals=0),
        )(*args)

    return call


def pack_kernel(side, feat, planes, gy_a, gy_b, gx_a, gx_b, c_aa, c_ab, c_ba, c_bb):
    step = pl.program_id(0)
    count = feat.shape[1]
    row, col = iota((256, 256), 0), iota((256, 256), 1)
    match = ((row >> 4) == (col & 15)) & ((row & 15) == (col >> 4))
    swap = jnp.where(match, 1.0, 0.0).astype(BF16)
    rows_a = pl.multiple_of(side[2] * 224, 32)
    rows_b = pl.multiple_of(side[3] * 224, 32)
    for x in range(0, count, 2):
        both = jnp.concatenate(
            [feat[:, x].reshape(256, 128), feat[:, x + 1].reshape(256, 128)], axis=1
        )
        moved = dot(swap, both).astype(BF16)
        planes[x] = moved[:, :128]
        planes[x + 1] = moved[:, 128:]
    gy_a[...] = planes[:, pl.ds(rows_a, 32), :]
    gy_b[...] = planes[:, pl.ds(rows_b, 32), :]
    last = pl.num_programs(0) - 1
    for which, face, edges in ((0, gx_a, (c_aa, c_ab)), (1, gx_b, (c_ba, c_bb))):

        @pl.when(step == side[which] * last)
        def _():
            at = side[which] * (count - 2)
            face[...] = planes[pl.ds(at, 2)]
            edges[0][...] = planes[pl.ds(at, 2), pl.ds(rows_a, 32), :]
            edges[1][...] = planes[pl.ds(at, 2), pl.ds(rows_b, 32), :]


def pack(side, features):
    size_x = features.shape[1]
    step = 8

    def fixed(*dims):
        return pl.BlockSpec(dims, lambda i: (0,) * len(dims))

    def shape(*dims):
        return jax.ShapeDtypeStruct(dims, BF16)

    return pl.pallas_call(
        pack_kernel,
        grid=(size_x // step,),
        in_specs=[
            pl.BlockSpec(memory_space=pltpu.SMEM),
            pl.BlockSpec((16, step, 16, 128), lambda i: (0, i, 0, 0)),
        ],
        out_specs=[pl.BlockSpec((step, 256, 128), lambda i: (i, 0, 0))]
        + [pl.BlockSpec((step, 32, 128), lambda i: (i, 0, 0))] * 2
        + [fixed(2, 256, 128)] * 2
        + [fixed(2, 32, 128)] * 4,
        out_shape=[shape(size_x, 256, 128)]
        + [shape(size_x, 32, 128)] * 2
        + [shape(2, 256, 128)] * 2
        + [shape(2, 32, 128)] * 4,
        cost_estimate=pl.CostEstimate(
            flops=2 * 256 * 256 * 128 * size_x, bytes_accessed=5 << 20, transcendentals=0
        ),
    )(side, features)


def band(w_ref, t_ref, block):
    rows, cols = 16 * block, 16 * (block + 2)
    spread = jnp.where((iota((16, cols), 1) & 15) == iota((16, cols), 0), 1.0, 0.0).astype(BF16)
    expand = jnp.where((iota((rows, 16), 0) & 15) == iota((rows, 16), 1), 1.0, 0.0).astype(BF16)
    delta = (iota((rows, cols), 1) >> 4) - (iota((rows, cols), 0) >> 4)
    for off_c in range(3):
        for off_a in range(3):
            total = jnp.zeros((rows, cols), F32)
            for off_b in range(3):
                tall = dot(expand, w_ref[9 * off_a + 3 * off_b + off_c]).astype(BF16)
                total = jnp.where(delta == off_b, dot(tall, spread), total)
            t_ref[off_c * rows : (off_c + 1) * rows, off_a * cols : (off_a + 1) * cols] = (
                total.astype(BF16)
            )


def prep_kernel(w1, w2, t1, t2, t2_last):
    band(w1, t1, 3)
    band(w2, t2, 3)
    band(w2, t2_last, 1)


def shifted_sum(acc, rows, half):
    lanes = slice(half * 128, half * 128 + 128)
    lane = iota((rows, 128), 1)
    before = pltpu.roll(acc[0:rows, lanes], 1, 1)
    after = pltpu.roll(acc[2 * rows : 3 * rows, lanes], 127, 1)
    total = acc[rows : 2 * rows, lanes]
    total = total + jnp.where(lane > 0, before, 0.0)
    total = total + jnp.where(lane < 127, after, 0.0)
    return jnp.maximum(total, 0.0)


def window(planes, at, row, rows):
    return jnp.concatenate(
        [
            jnp.concatenate([planes[at + h + a, row : row + rows] for a in range(3)], axis=0)
            for h in range(2)
        ],
        axis=1,
    )


def conv_kernel(
    planes, gy_a, gy_b, gx_a, gx_b, c_aa, c_ab, c_ba, c_bb, masks, t1, t2, t2_last,
    second, pooled, fe, f1, f2, psum, sems,
):
    size_x = planes.shape[0]
    flags = [masks[i : i + 1, :] for i in range(8)]
    x_sides = (flags[0:2], flags[2:4])
    y_sides = (flags[4:6], flags[6:8])

    def mix(a, b, flag_a, flag_b):
        return (a.astype(F32) * flag_a + b.astype(F32) * flag_b).astype(BF16)

    def scaled(v, m):
        return (v.astype(F32) * m).astype(BF16)

    def fill(x, carry):
        fe[x + 2, 32:288] = planes[x]
        fe[x + 2, 0:32] = mix(gy_a[x], gy_b[x], *y_sides[0])
        fe[x + 2, 288:320] = mix(gy_a[x], gy_b[x], *y_sides[1])
        return carry

    lax.fori_loop(0, size_x, fill, 0, unroll=2)
    for (x_a, x_b), base in zip(x_sides, (0, size_x + 2)):
        for j in range(2):
            fe[base + j, 32:288] = mix(gx_a[j], gx_b[j], x_a, x_b)
            for (y_a, y_b), row in zip(y_sides, (0, 288)):
                total = c_aa[j].astype(F32) * (x_a * y_a) + c_ab[j].astype(F32) * (x_a * y_b)
                total = total + c_ba[j].astype(F32) * (x_b * y_a)
                total = total + c_bb[j].astype(F32) * (x_b * y_b)
                fe[base + j, row : row + 32] = total.astype(BF16)

    y_left, y_right = y_sides[0][0] + y_sides[0][1], y_sides[1][0] + y_sides[1][1]

    def conv_one(p, carry):
        at = 2 * p
        for j in range(6):
            acc = dot(t1[...], window(fe, at, 48 * j, 80))
            for h in range(2):
                value = shifted_sum(acc, 48, h)
                if j == 0:
                    value = jnp.concatenate([value[:16] * y_left, value[16:]], axis=0)
                if j == 5:
                    value = jnp.concatenate([value[:32], value[32:] * y_right], axis=0)
                f1[at + h, 48 * j : 48 * j + 48] = value.astype(BF16)
        return carry

    lax.fori_loop(0, (size_x + 2) // 2, conv_one, 0)
    f1[0] = scaled(f1[0], x_sides[0][0] + x_sides[0][1])
    f1[size_x + 1] = scaled(f1[size_x + 1], x_sides[1][0] + x_sides[1][1])

    def copy(q):
        return pltpu.make_async_copy(
            f2.at[pl.ds(2 * q, 2)], second.at[pl.ds(2 * q, 2)], sems.at[q]
        )

    psum[...] = jnp.zeros(psum.shape, F32)

    def conv_two(q, carry):
        at = 2 * q
        summed = jnp.zeros((16, 128), F32)
        for j in range(6):
            if j < 5:
                rows = 48
                acc = dot(t2[...], window(f1, at, 48 * j, 80))
            else:
                rows = 16
                acc = dot(t2_last[...], window(f1, at, 240, 48))
            for h in range(2):
                value = shifted_sum(acc, rows, h).astype(BF16)
                f2[at + h, 48 * j : 48 * j + rows] = value
                summed = summed + jnp.sum(
                    value.astype(F32).reshape(rows // 16, 16, 128), axis=0
                )
        block = q // (POOL // 2)
        psum[block] += summed
        copy(q).start()
        return carry

    lax.fori_loop(0, size_x // 2, conv_two, 0)
    z, lane = iota((128, 128), 0), iota((128, 128), 1)
    gather = jnp.where((z >> 4) == (lane & 7), 1.0, 0.0).astype(F32)
    keep = (iota((16, 128), 1) >> 3) == iota((16, 128), 0)
    results = []
    for block in range(size_x // POOL):
        cells = jnp.dot(
            psum[block], gather, preferred_element_type=F32, precision=lax.Precision.HIGHEST
        )
        row = jnp.sum(jnp.where(keep, cells, 0.0), axis=0, keepdims=True) * (1.0 / POOL**3)
        results.append(row)
    both = jnp.concatenate(results, axis=0)
    for d in range(16):
        pooled[d] = both

    def finish(q, carry):
        copy(q).wait()
        return carry

    lax.fori_loop(0, size_x // 2, finish, 0)


def convolve(args, size_x):
    vmem = pl.BlockSpec(memory_space=pltpu.VMEM)
    return pl.pallas_call(
        conv_kernel,
        in_specs=[vmem] * len(args),
        out_specs=[pl.BlockSpec(memory_space=pl.ANY), vmem],
        out_shape=[
            jax.ShapeDtypeStruct((size_x, 256, 128), BF16),
            jax.ShapeDtypeStruct((16, 2, 128), F32),
        ],
        scratch_shapes=[
            pltpu.VMEM((size_x + 4, 320, 128), BF16),
            pltpu.VMEM((size_x + 2, 288, 128), BF16),
            pltpu.VMEM((size_x, 256, 128), BF16),
            pltpu.VMEM((size_x // POOL, 16, 128), F32),
            pltpu.SemaphoreType.DMA((size_x // 2,)),
        ],
        cost_estimate=pl.CostEstimate(
            flops=2 * 2 * 864 * 256 * 128 * size_x, bytes_accessed=6 << 20, transcendentals=0
        ),
    )(*args)


def split3(v):
    a = v.astype(BF16)
    v = v - a.astype(F32)
    b = v.astype(BF16)
    c = (v - b.astype(F32)).astype(BF16)
    return a, b, c


def swap_groups(rows):
    lane = iota((256, 128), 1)
    major, minor = iota((256, 128), 0) >> 4, iota((256, 128), 0) & 15
    spread = jnp.broadcast_to(rows[:, None, :], (16, 16, 128)).reshape(256, 128)
    spread = jnp.where((lane >> 3) == minor, spread, 0.0)
    l0, l1 = iota((128, 128), 0), iota((128, 128), 1)
    fold = jnp.where((l0 & 7) == (l1 & 7), 1.0, 0.0).astype(BF16)
    out = []
    for piece in split3(spread):
        moved = jnp.where((lane >> 3) == major, dot(piece, fold), 0.0)
        out.append(jnp.sum(moved.reshape(16, 16, 128), axis=0))
    return out


def coarse_kernel(own, gl, gr, masks, w_lift, w_coarse, w_dec, out):
    m_xl, m_xr = masks[0:1, :], masks[1:2, :]
    slabs = [gl[...] * m_xl, own[:, 0, :], own[:, 1, :], gr[...] * m_xr]
    columns = []
    for slab in slabs:
        pieces = [v.astype(BF16) for v in swap_groups(slab)]
        columns.append(jnp.concatenate(pieces, axis=0))
    stacked = jnp.concatenate(columns, axis=1)
    lift = w_lift[...]
    lift3 = jnp.concatenate([lift, lift, lift], axis=1)
    lifted = jnp.maximum(dot(lift3, stacked), 0.0).astype(BF16)
    count = w_dec.shape[1]
    partial = dot(w_coarse[...], lifted)
    lane = iota((count, 128), 1)
    y, z = lane >> 3, lane & 7
    for x in range(2):
        total = jnp.zeros((count, 128), F32)
        for k in range(27):
            a, b, c = k // 9, k // 3 % 3 - 1, k % 3 - 1
            piece = partial[k * count : (k + 1) * count, (x + a) * 128 : (x + a) * 128 + 128]
            step = 8 * b + c
            if step:
                piece = pltpu.roll(piece, (-step) % 128, 1)
            good = None
            if b:
                good = (y < 15) if b > 0 else (y > 0)
            if c:
                inside = (z < 7) if c > 0 else (z > 0)
                good = inside if good is None else good & inside
            total = total + (piece if good is None else jnp.where(good, piece, 0.0))
        coarse = jnp.maximum(total, 0.0).astype(BF16)
        part = dot(w_dec[...], coarse)
        pieces = swap_groups(part)
        out[:, x, :] = pieces[0] + pieces[1] + pieces[2]


def join_kernel(second, parts, w_join, out, matrix, term):
    @pl.when(pl.program_id(0) == 0)
    def _():
        r, c = iota((256, 16), 0), iota((256, 16), 1)
        rows = jnp.where((r >> 4) == c, 1.0, 0.0).astype(BF16)
        mixed = dot(rows, w_join[...]).astype(BF16)
        r, c = iota((16, 256), 0), iota((16, 256), 1)
        cols = jnp.where((c & 15) == r, 1.0, 0.0).astype(BF16)
        r, c = iota((256, 256), 0), iota((256, 256), 1)
        matrix[...] = jnp.where((r & 15) == (c >> 4), dot(mixed[:, 0:16], cols), 0.0).astype(BF16)
        keep = (iota((16, 128), 1) >> 3) == iota((16, 128), 0)
        l0, l1 = iota((128, 128), 0), iota((128, 128), 1)
        widen = jnp.where((l0 & 7) == (l1 >> 4), 1.0, 0.0).astype(BF16)
        total = parts[0]
        for d in range(1, 16):
            total = total + parts[d]
        for block in range(2):
            decoded = jnp.broadcast_to(total[block : block + 1, :], (16, 128))
            decoded = jnp.where(keep, decoded, 0.0).astype(BF16)
            term[block] = dot(mixed[:, 16:32], dot(decoded, widen).astype(BF16))

    count = second.shape[0]
    value = term[pl.program_id(0) * count // POOL]
    value = jnp.concatenate([value, value], axis=1)
    for x in range(0, count, 2):
        both = jnp.concatenate([second[x], second[x + 1]], axis=1)
        result = (dot(matrix[...], both) + value).astype(BF16)
        for h in range(2):
            out[:, x + h] = result[:, h * 128 : h * 128 + 128].reshape(16, 16, 128)


def join(second, parts, w_join):
    size_x = second.shape[0]
    step = 8
    return pl.pallas_call(
        join_kernel,
        grid=(size_x // step,),
        in_specs=[
            pl.BlockSpec((step, 256, 128), lambda i: (i, 0, 0)),
            pl.BlockSpec((16, 2, 128), lambda i: (0, 0, 0)),
            pl.BlockSpec((16, 32), lambda i: (0, 0)),
        ],
        out_specs=pl.BlockSpec((16, step, 16, 128), lambda i: (0, i, 0, 0)),
        out_shape=jax.ShapeDtypeStruct((16, size_x, 16, 128), BF16),
        scratch_shapes=[pltpu.VMEM((256, 256), BF16), pltpu.VMEM((2, 256, 128), F32)],
        cost_estimate=pl.CostEstimate(
            flops=2 * 256 * 256 * 128 * size_x, bytes_accessed=4 << 20, transcendentals=0
        ),
    )(second, parts, w_join)


def local(features, w_first, w_second, w_lift, w_coarse, w_decode, w_joining):
    size_x = features.shape[1]
    nx, ny = lax.axis_size("gx"), lax.axis_size("gy")
    gx, gy = lax.axis_index("gx"), lax.axis_index("gy")

    def ring(count, step):
        return [(i, (i + step) % count) for i in range(count)]

    def swap(count, odd):
        return [(((i + odd) ^ 1) - odd) % count for i in range(count)]

    def shape(*dims, dtype=BF16):
        return jax.ShapeDtypeStruct(dims, dtype)

    even_x, even_y = gx % 2 == 0, gy % 2 == 0
    side = jnp.stack([even_x, ~even_x, even_y, ~even_y]).astype(jnp.int32)
    row = lax.broadcasted_iota(jnp.int32, (8, 128), 0)
    flags = [
        ~even_x, even_x & (gx > 0), even_x, ~even_x & (gx < nx - 1),
        ~even_y, even_y & (gy > 0), even_y, ~even_y & (gy < ny - 1),
    ]
    edges = [gx > 0, gx < nx - 1]
    masks = jnp.zeros((8, 128), jnp.bool_)
    for i, flag in enumerate(flags):
        masks = jnp.where(row == i, flag, masks)
    masks = masks.astype(F32)
    ends = jnp.where(row == 0, edges[0], edges[1]).astype(F32)

    planes, gy_a, gy_b, gx_a, gx_b, *corners = pack(side, features)
    across = {"x": [swap(nx, 0), swap(nx, 1)], "y": [swap(ny, 0), swap(ny, 1)]}

    def along(value, axis, to):
        return lax.ppermute(value, axis, list(enumerate(to)))

    def diagonal(value, to_x, to_y):
        pairs = [
            (i * ny + j, to_x[i] * ny + to_y[j]) for i in range(nx) for j in range(ny)
        ]
        return lax.ppermute(value, ("gx", "gy"), pairs)

    gy_a, gy_b = along(gy_a, "gy", across["y"][0]), along(gy_b, "gy", across["y"][1])
    gx_a, gx_b = along(gx_a, "gx", across["x"][0]), along(gx_b, "gx", across["x"][1])
    corners = [
        diagonal(corners[2 * i + j], across["x"][i], across["y"][j])
        for i in range(2)
        for j in range(2)
    ]

    t1, t2, t2_last = vmem_call(
        prep_kernel,
        [shape(144, 240), shape(144, 240), shape(48, 144)],
        flops=1 << 27,
        nbytes=1 << 20,
    )(w_first, w_second)
    count = w_coarse.shape[0]
    w_rows = jnp.transpose(w_coarse, (1, 0, 2)).reshape(27 * count, w_coarse.shape[2])
    w_dec = lax.dynamic_slice_in_dim(w_decode, gy * count, count, axis=1)

    second, pooled = convolve(
        (planes, gy_a, gy_b, gx_a, gx_b, *corners, masks, t1, t2, t2_last), size_x
    )

    gathered = lax.all_to_all(pooled, "gy", 0, 0)
    gl = lax.ppermute(gathered[:, 1, :], "gx", ring(nx, 1))
    gr = lax.ppermute(gathered[:, 0, :], "gx", ring(nx, -1))
    parts = vmem_call(
        coarse_kernel,
        shape(16, 2, 128, dtype=F32),
        flops=2 * 864 * 512 * 512,
        nbytes=2 << 20,
    )(gathered, gl, gr, ends, w_lift, w_rows, w_dec)
    parts = lax.all_to_all(parts, "gy", 0, 0)
    return join(second, parts, w_joining)


def solution(mesh):
    in_specs = (P(None, "gx", "gy", None), P(), P(), P(), P("gy", None, None), P(), P())
    out_specs = P(None, "gx", "gy", None)
    return jax.shard_map(local, mesh=mesh, in_specs=in_specs, out_specs=out_specs, check_vma=False)
```

time: 101 us -> 87.2 us (0.86)
  Pallas kernels: 47.9 us -> 31.9 us
  starting transfers between devices: 24.7 us -> 32.1 us
  waiting for transfers between devices: 12.1 us -> 6.06 us
    pallas_call x5 -> x2, Pallas kernels: 47.9 us -> 6.27 us  [call(): pl.pallas_call(kernel, out_shape=out_shape, in_specs=[pl.BlockSpec(memory...]
    pallas_call x0 -> x3, Pallas kernels: none -> 25.7 us  [the longest x1 16.3 us: convolve(): pl.pallas_call(conv_kernel, in_specs=[vmem] * len(args), out_specs=[pl.Bl...]
    ppermute x6 -> x8, starting transfers between devices: 12.3 us -> 20.9 us  [the longest x4 12.9 us: diagonal(): return lax.ppermute(value, ('gx', 'gy'), pairs)]
    ppermute x6 -> x8, waiting for transfers between devices: 6.32 us -> 0.68 us  [the longest x4 0.67 us: diagonal(): return lax.ppermute(value, ('gx', 'gy'), pairs)]
    all_to_all x1, starting transfers between devices: 7.32 us -> 6.06 us  [local(): gathered = lax.all_to_all(pooled, 'gy', 0, 0)]
    unnamed x29 -> x33, local copies, waits for them, and re-layouts: 3.05 us -> 2.49 us
  transfers between devices with their start and end apart: 9 -> 11, of which waited for: 3 -> 4; matrix products, arithmetic and copies ran while one was open for 3% -> 4% of each run, Pallas kernels for 5% -> 3%
where the time goes in v1:
time: 87.2 us; the launch traced here: 86.8 us
  starting transfers between devices  32.1 us (37%)
  Pallas kernels  31.9 us (37%)
  blocking collectives  11.3 us (13%)
  waiting for transfers between devices  6.06 us (7%)
  local copies, waits for them, and re-layouts  4.63 us (5%)
    pallas_call x1, Pallas kernels, convolve(): pl.pallas_call(conv_kernel, in_specs=[vmem] * len(args), out_specs=[pl.Bl...  16.3 us
    ppermute x4, starting transfers between devices, diagonal(): return lax.ppermute(value, ('gx', 'gy'), pairs)  12.9 us
    all_to_all x1, blocking collectives, local(): parts = lax.all_to_all(parts, 'gy', 0, 0)  11.3 us
    ppermute x4, starting transfers between devices, along(): return lax.ppermute(value, axis, list(enumerate(to)))  8.01 us
    pallas_call x2, Pallas kernels, call(): pl.pallas_call(kernel, out_shape=out_shape, in_specs=[pl.BlockSpec(memory...  6.27 us
    all_to_all x1, starting transfers between devices, local(): gathered = lax.all_to_all(pooled, 'gy', 0, 0)  6.06 us
    all_to_all x1, waiting for transfers between devices, local(): gathered = lax.all_to_all(pooled, 'gy', 0, 0)  5.11 us
    ppermute x1, starting transfers between devices, local(): gr = lax.ppermute(gathered[:, 0, :], 'gx', ring(nx, -1))  5.07 us
  transfers between devices with their start and end apart: 11, of which 4 were waited for; matrix products, arithmetic and copies ran while one was open for 4% of the time, Pallas kernels for 3%

profile of v1, /device:TPU:1, one launch (start us, length us, event | category | flops | bytes accessed | tf_op | source)
XLA Modules:
  0.0 86.8 jit_solution(16087780780581951006)
XLA Ops:
  0.0 0.0 copy-start
  0.0 0.0 copy-start.2
  0.0 0.0 copy-start.3
  0.0 0.6 add_convert_fusion.side
  0.6 4.6 %shard_map.73 = (bf16[32,256,128]{2,1,0:T(8,128)(2,1)}, bf16[32,32,128]{2,1,0:T(8,128)(2,1)}, bf16[32,32,128]{2,1,0:T(8,128)(2,1)}, bf16[2,256,128]{2,1,0:T(8,12...) custom-call(s32[4]{0:T(128)} %add_convert_fusion.side, ...), custom_call_target="tpu_custom_call" | custom-call | flops 536870912 | bytes 5242880 | tf_op jit(solution)/shard_map/pallas_call | solution.py:79
  5.2 1.4 %collective-permute-start = (bf16[32,32,128]{2,1,0:T(8,128)(2,1)}, bf16[32,32,128]{2,1,0:T(8,128)(2,1)S(1)}, u32[]{:S(2)}, u32[]{:S(2)}) collective-permute-start(bf16[32,32,128]{2,1,0:T(8,128)(2,1)} %get-tuple-element.20), channel_id=1, source_target_pairs={{0,1},{1,0},{2,3},{3,2},{4,5},{5,4},{6,7},{7,6},{8,9},{9,8},{10,11... | collective-permute-start | bytes 786440 | tf_op jit(solution)/shard_map/ppermute | solution.py:407
  6.6 1.4 %collective-permute-start.1 = (bf16[32,32,128]{2,1,0:T(8,128)(2,1)}, bf16[32,32,128]{2,1,0:T(8,128)(2,1)S(1)}, u32[]{:S(2)}, u32[]{:S(2)}) collective-permute-start(bf16[32,32,128]{2,1,0:T(8,128)(2,1)} %get-tuple-element.21), channel_id=1, source_target_pairs={{0,15},{1,2},{2,1},{3,4},{4,3},{5,6},{6,5},{7,8},{8,7},{9,10},{10,... | collective-permute-start | bytes 786440 | tf_op jit(solution)/shard_map/ppermute | solution.py:407
  8.0 6.4 %collective-permute-start.4 = (bf16[2,32,128]{2,1,0:T(8,128)(2,1)}, bf16[2,32,128]{2,1,0:T(8,128)(2,1)S(1)}, u32[]{:S(2)}, u32[]{:S(2)}) collective-permute-start(bf16[2,32,128]{2,1,0:T(8,128)(2,1)} %get-tuple-element.24), channel_id=1, source_target_pairs={{0,17},{1,16},{2,19},{3,18},{4,21},{5,20},{6,23},{7,22},{8,25},{9,... | collective-permute-start | bytes 49160 | tf_op jit(solution)/shard_map/ppermute | solution.py:413
  14.4 0.0 collective-permute-start.5
  14.4 4.1 %collective-permute-start.6 = (bf16[2,32,128]{2,1,0:T(8,128)(2,1)}, bf16[2,32,128]{2,1,0:T(8,128)(2,1)S(1)}, u32[]{:S(2)}, u32[]{:S(2)}) collective-permute-start(bf16[2,32,128]{2,1,0:T(8,128)(2,1)} %get-tuple-element.26), channel_id=1, source_target_pairs={{0,113},{1,112},{2,115},{3,114},{4,117},{5,116},{6,119},{7,118},{8... | collective-permute-start | bytes 49160 | tf_op jit(solution)/shard_map/ppermute | solution.py:413
  18.5 0.6 collective-permute-done.4.c_aa
  19.1 0.0 copy-start.9
  19.1 0.5 collective-permute-start.2
  19.7 0.0 collective-permute-done.5.c_ab
  19.7 0.0 copy-start.10
  19.7 4.6 %collective-permute-start.3 = (bf16[2,256,128]{2,1,0:T(8,128)(2,1)}, bf16[2,256,128]{2,1,0:T(8,128)(2,1)S(1)}, u32[]{:S(2)}, u32[]{:S(2)}) collective-permute-start(bf16[2,256,128]{2,1,0:T(8,128)(2,1)} %get-tuple-element.23), channel_id=1, source_target_pairs={{0,112},{16,32},{32,16},{48,64},{64,48},{80,96},{96,80},{112,0},{1... | collective-permute-start | bytes 393224 | tf_op jit(solution)/shard_map/ppermute | solution.py:407
  24.3 0.0 collective-permute-done.6.c_ba
  24.3 0.0 copy-start.11
  24.3 2.4 %collective-permute-start.7 = (bf16[2,32,128]{2,1,0:T(8,128)(2,1)}, bf16[2,32,128]{2,1,0:T(8,128)(2,1)S(1)}, u32[]{:S(2)}, u32[]{:S(2)}) collective-permute-start(bf16[2,32,128]{2,1,0:T(8,128)(2,1)} %get-tuple-element.27), channel_id=1, source_target_pairs={{0,127},{1,114},{2,113},{3,116},{4,115},{5,118},{6,117},{7,120},{8... | collective-permute-start | bytes 49160 | tf_op jit(solution)/shard_map/ppermute | solution.py:413
  26.7 0.0 copy-done.2
  26.7 0.8 copy.13.w1
  27.5 0.0 copy-done.3
  27.5 0.8 copy.14.w2
  28.4 2.7 %shard_map.74 = (bf16[144,240]{1,0:T(8,128)(2,1)}, bf16[144,240]{1,0:T(8,128)(2,1)}, bf16[48,144]{1,0:T(8,128)(2,1)}) custom-call(bf16[27,16,16]{2,1,0:T(8,128)(2,1)} %copy.13.w1, bf16[27,16,16]{2,1,0:T(8,128)(2,1)} %copy.14.w2), custom_call_target="tpu_custom_call" | custom-call | flops 134217728 | bytes 1048576 | tf_op jit(solution)/shard_map/pallas_call | solution.py:25
  31.0 0.1 collective-permute-done.7.c_bb
  31.1 0.0 copy-start.12
  31.1 0.0 collective-permute-done.2.gx_a
  31.1 0.0 copy-start.7
  31.1 0.0 collective-permute-done.3.gx_b
  31.1 0.0 copy-start.8
  31.1 0.0 collective-permute-done.gy_a
  31.1 0.0 copy-start.5
  31.2 0.0 collective-permute-done.1.gy_b
  31.2 0.0 copy-start.6
  31.2 0.8 iota.32.masks
  32.0 0.0 copy-done.9
  32.0 0.0 copy-done.10
  32.0 0.0 copy-done.11
  32.0 0.0 copy-done.12
  32.0 0.0 copy-done.7
  32.0 0.0 copy-done.8
  32.0 0.0 copy-done.5
  32.0 0.0 copy-done.6
  32.0 0.0 copy-start.4
  32.0 16.3 %shard_map.75 = (bf16[32,256,128]{2,1,0:T(8,128)(2,1)}, f32[16,2,128]{2,1,0:T(2,128)}) custom-call(bf16[32,256,128]{2,1,0:T(8,128)(2,1)} %get-tuple-element.19.planes, bf16[32,32,128]{2,1,0:T(8,128)(2,1)} %copy-done.5, bf16[32,32,128]{2,1,0:T(8,128)(2,1)} %copy-done.6, bf16[2,256,128]{2,1,0:T(8,128)(2,1)} %copy-done.7, bf16[2,256,128]{2,1,0:T(8,128)(2,1)} %copy-done.8, ...), custom_call_target="tpu_custom_call" | custom-call | flops 3623878656 | bytes 6291456 | tf_op jit(solution)/shard_map/pallas_call | solution.py:245
  48.4 6.1 %all-to-all-start = ((f32[16,2,128]{2,1,0:T(2,128)}), f32[16,2,128]{2,1,0:T(2,128)S(1)}, u32[]{:S(2)}, u32[]{:S(2)}) async-start(f32[16,2,128]{2,1,0:T(2,128)} %get-tuple-element.32), calls=%async_computation | async-start | bytes 32768 | tf_op jit(solution)/shard_map/all_to_all | solution.py:437
  54.4 0.0 copy-done
  54.4 0.7 constant_dynamic-slice_fusion.w_dec
  55.1 5.1 %all-to-all-done.own = f32[16,2,128]{2,1,0:T(2,128)S(1)} async-done(((f32[16,2,128]{2,1,0:T(2,128)}), f32[16,2,128]{2,1,0:T(2,128)S(1)}, u32[]{:S(2)}, u32[]{:S(2)}) %all-to-all-start) | async-done | bytes 16416 | tf_op jit(solution)/shard_map/all_to_all | solution.py:437
  60.2 0.0 copy-start.1
  60.2 0.1 collective-permute-start.8
  60.3 5.1 %collective-permute-start.9 = (f32[16,128]{1,0:T(8,128)S(1)}, f32[16,128]{1,0:T(8,128)S(1)}, u32[]{:S(2)}, u32[]{:S(2)}) collective-permute-start(f32[16,128]{1,0:T(8,128)S(1)} %bitcast.13), channel_id=1, source_target_pairs={{0,112},{16,0},{32,16},{48,32},{64,48},{80,64},{96,80},{112,96},{1... | collective-permute-start | bytes 24584 | tf_op jit(solution)/shard_map/ppermute | solution.py:439
  65.4 0.0 copy-done.4
  65.4 0.8 copy.17.w_lift
  66.2 0.3 collective-permute-done.8.gl
  66.4 0.0 copy-start.13
  66.4 0.0 collective-permute-done.9.gr
  66.4 0.7 iota.33.masks
  67.1 0.0 copy-done.1
  67.1 0.0 copy-done.13
  67.1 0.0 copy-done.14
  67.1 3.6 %shard_map.76 = f32[16,2,128]{2,1,0:T(2,128)} custom-call(f32[16,2,128]{2,1,0:T(2,128)} %copy-done.1, f32[16,128]{1,0:T(8,128)} %copy-done.13, f32[16,128]{1,0:T(8,128)} %copy-done.14, f32[8,128]{1,0:T(8,128)} %iota.33.masks, bf16[512,16]{1,0:T(8,128)(2,1)} %copy.17.w_lift, bf16[864,512]{1,0:T(8,128)(2,1)} %bitcast.15, ...), custom_call_target="tpu_custom_call" | custom-call | flops 452984832 | bytes 2097152 | tf_op jit(solution)/shard_map/pallas_call | solution.py:25
  70.7 11.3 %all_to_all.10.parts = f32[16,2,128]{2,1,0:T(2,128)} all-to-all(f32[16,2,128]{2,1,0:T(2,128)} %shard_map.76), channel_id=1, replica_groups=mesh['gx'=8,'gy'=16] {'gy'}, dimensions={0} | all-to-all | bytes 32768 | tf_op jit(solution)/shard_map/all_to_all | solution.py:446
  82.0 4.8 %shard_map.77 = bf16[16,32,16,128]{3,2,1,0:T(8,128)(2,1)} custom-call(bf16[32,256,128]{2,1,0:T(8,128)(2,1)} %get-tuple-element.31.second, f32[16,2,128]{2,1,0:T(2,128)} %all_to_all.10.parts, bf16[16,32]{1,0:T(8,128)(2,1)} %w_join.1), custom_call_target="tpu_custom_call" | custom-call | flops 536870912 | bytes 4194304 | tf_op jit(solution)/shard_map/pallas_call | solution.py:358
  (4 shorter events, 0.0 us)
Async XLA Ops:
  0.0 54.4 %copy-start = (bf16[16,512]{1,0:T(8,128)(2,1)S(1)}, bf16[16,512]{1,0:T(8,128)(2,1)}, u32[]{:S(2)}) copy-start(bf16[16,512]{1,0:T(8,128)(2,1)} %param.12) | copy-start | bytes 49156
  0.0 26.7 %copy-start.2 = (bf16[27,16,16]{0,2,1:T(8,128)(2,1)S(1)}, bf16[27,16,16]{0,2,1:T(8,128)(2,1)}, u32[]{:S(2)}) copy-start(bf16[27,16,16]{0,2,1:T(8,128)(2,1)} %param.8) | copy-start | bytes 41476
  0.0 27.5 %copy-start.3 = (bf16[27,16,16]{0,2,1:T(8,128)(2,1)S(1)}, bf16[27,16,16]{0,2,1:T(8,128)(2,1)}, u32[]{:S(2)}) copy-start(bf16[27,16,16]{0,2,1:T(8,128)(2,1)} %param.9) | copy-start | bytes 41476
  5.2 26.0 %collective-permute-start = (bf16[32,32,128]{2,1,0:T(8,128)(2,1)}, bf16[32,32,128]{2,1,0:T(8,128)(2,1)S(1)}, u32[]{:S(2)}, u32[]{:S(2)}) collective-permute-start(bf16[32,32,128]{2,1,0:T(8,128)(2,1)} %get-tuple-element.20), channel_id=1, source_target_pairs={{0,1},{1,0},{2,3},{3,2},{4,5},{5,4},{6,7},{7,6},{8,9},{9,8},{10,11... | collective-permute-start | bytes 786440 | tf_op jit(solution)/shard_map/ppermute | solution.py:407
  6.6 24.6 %collective-permute-start.1 = (bf16[32,32,128]{2,1,0:T(8,128)(2,1)}, bf16[32,32,128]{2,1,0:T(8,128)(2,1)S(1)}, u32[]{:S(2)}, u32[]{:S(2)}) collective-permute-start(bf16[32,32,128]{2,1,0:T(8,128)(2,1)} %get-tuple-element.21), channel_id=1, source_target_pairs={{0,15},{1,2},{2,1},{3,4},{4,3},{5,6},{6,5},{7,8},{8,7},{9,10},{10,... | collective-permute-start | bytes 786440 | tf_op jit(solution)/shard_map/ppermute | solution.py:407
  8.0 11.1 %collective-permute-start.4 = (bf16[2,32,128]{2,1,0:T(8,128)(2,1)}, bf16[2,32,128]{2,1,0:T(8,128)(2,1)S(1)}, u32[]{:S(2)}, u32[]{:S(2)}) collective-permute-start(bf16[2,32,128]{2,1,0:T(8,128)(2,1)} %get-tuple-element.24), channel_id=1, source_target_pairs={{0,17},{1,16},{2,19},{3,18},{4,21},{5,20},{6,23},{7,22},{8,25},{9,... | collective-permute-start | bytes 49160 | tf_op jit(solution)/shard_map/ppermute | solution.py:413
  14.4 5.3 %collective-permute-start.5 = (bf16[2,32,128]{2,1,0:T(8,128)(2,1)}, bf16[2,32,128]{2,1,0:T(8,128)(2,1)S(1)}, u32[]{:S(2)}, u32[]{:S(2)}) collective-permute-start(bf16[2,32,128]{2,1,0:T(8,128)(2,1)} %get-tuple-element.25), channel_id=1, source_target_pairs={{0,31},{1,18},{2,17},{3,20},{4,19},{5,22},{6,21},{7,24},{8,23},{9,... | collective-permute-start | bytes 49160 | tf_op jit(solution)/shard_map/ppermute | solution.py:413
  14.4 9.9 %collective-permute-start.6 = (bf16[2,32,128]{2,1,0:T(8,128)(2,1)}, bf16[2,32,128]{2,1,0:T(8,128)(2,1)S(1)}, u32[]{:S(2)}, u32[]{:S(2)}) collective-permute-start(bf16[2,32,128]{2,1,0:T(8,128)(2,1)} %get-tuple-element.26), channel_id=1, source_target_pairs={{0,113},{1,112},{2,115},{3,114},{4,117},{5,116},{6,119},{7,118},{8... | collective-permute-start | bytes 49160 | tf_op jit(solution)/shard_map/ppermute | solution.py:413
  19.1 12.9 %copy-start.9 = (bf16[2,32,128]{2,1,0:T(8,128)(2,1)}, bf16[2,32,128]{2,1,0:T(8,128)(2,1)S(1)}, u32[]{:S(2)}) copy-start(bf16[2,32,128]{2,1,0:T(8,128)(2,1)S(1)} %collective-permute-done.4.c_aa) | copy-start | bytes 49156
  19.1 12.0 %collective-permute-start.2 = (bf16[2,256,128]{2,1,0:T(8,128)(2,1)}, bf16[2,256,128]{2,1,0:T(8,128)(2,1)S(1)}, u32[]{:S(2)}, u32[]{:S(2)}) collective-permute-start(bf16[2,256,128]{2,1,0:T(8,128)(2,1)} %get-tuple-element.22), channel_id=1, source_target_pairs={{0,16},{16,0},{32,48},{48,32},{64,80},{80,64},{96,112},{112,96},{1... | collective-permute-start | bytes 393224 | tf_op jit(solution)/shard_map/ppermute | solution.py:407
  19.7 12.3 %copy-start.10 = (bf16[2,32,128]{2,1,0:T(8,128)(2,1)}, bf16[2,32,128]{2,1,0:T(8,128)(2,1)S(1)}, u32[]{:S(2)}) copy-start(bf16[2,32,128]{2,1,0:T(8,128)(2,1)S(1)} %collective-permute-done.5.c_ab) | copy-start | bytes 49156
  19.7 11.4 %collective-permute-start.3 = (bf16[2,256,128]{2,1,0:T(8,128)(2,1)}, bf16[2,256,128]{2,1,0:T(8,128)(2,1)S(1)}, u32[]{:S(2)}, u32[]{:S(2)}) collective-permute-start(bf16[2,256,128]{2,1,0:T(8,128)(2,1)} %get-tuple-element.23), channel_id=1, source_target_pairs={{0,112},{16,32},{32,16},{48,64},{64,48},{80,96},{96,80},{112,0},{1... | collective-permute-start | bytes 393224 | tf_op jit(solution)/shard_map/ppermute | solution.py:407
  24.3 7.7 %copy-start.11 = (bf16[2,32,128]{2,1,0:T(8,128)(2,1)}, bf16[2,32,128]{2,1,0:T(8,128)(2,1)S(1)}, u32[]{:S(2)}) copy-start(bf16[2,32,128]{2,1,0:T(8,128)(2,1)S(1)} %collective-permute-done.6.c_ba) | copy-start | bytes 49156
  24.3 6.8 %collective-permute-start.7 = (bf16[2,32,128]{2,1,0:T(8,128)(2,1)}, bf16[2,32,128]{2,1,0:T(8,128)(2,1)S(1)}, u32[]{:S(2)}, u32[]{:S(2)}) collective-permute-start(bf16[2,32,128]{2,1,0:T(8,128)(2,1)} %get-tuple-element.27), channel_id=1, source_target_pairs={{0,127},{1,114},{2,113},{3,116},{4,115},{5,118},{6,117},{7,120},{8... | collective-permute-start | bytes 49160 | tf_op jit(solution)/shard_map/ppermute | solution.py:413
  31.1 0.9 %copy-start.12 = (bf16[2,32,128]{2,1,0:T(8,128)(2,1)}, bf16[2,32,128]{2,1,0:T(8,128)(2,1)S(1)}, u32[]{:S(2)}) copy-start(bf16[2,32,128]{2,1,0:T(8,128)(2,1)S(1)} %collective-permute-done.7.c_bb) | copy-start | bytes 49156
  31.1 0.9 %copy-start.7 = (bf16[2,256,128]{2,1,0:T(8,128)(2,1)}, bf16[2,256,128]{2,1,0:T(8,128)(2,1)S(1)}, u32[]{:S(2)}) copy-start(bf16[2,256,128]{2,1,0:T(8,128)(2,1)S(1)} %collective-permute-done.2.gx_a) | copy-start | bytes 393220
  31.1 0.9 %copy-start.8 = (bf16[2,256,128]{2,1,0:T(8,128)(2,1)}, bf16[2,256,128]{2,1,0:T(8,128)(2,1)S(1)}, u32[]{:S(2)}) copy-start(bf16[2,256,128]{2,1,0:T(8,128)(2,1)S(1)} %collective-permute-done.3.gx_b) | copy-start | bytes 393220
  31.1 0.9 copy-start.5
  31.2 0.9 copy-start.6
  32.0 33.4 %copy-start.4 = (bf16[512,16]{0,1:T(8,128)(2,1)S(1)}, bf16[512,16]{0,1:T(8,128)(2,1)}, u32[]{:S(2)}) copy-start(bf16[512,16]{0,1:T(8,128)(2,1)} %param.10) | copy-start | bytes 49156
  48.4 11.9 %all-to-all-start = ((f32[16,2,128]{2,1,0:T(2,128)}), f32[16,2,128]{2,1,0:T(2,128)S(1)}, u32[]{:S(2)}, u32[]{:S(2)}) async-start(f32[16,2,128]{2,1,0:T(2,128)} %get-tuple-element.32), calls=%async_computation | async-start | bytes 32768 | tf_op jit(solution)/shard_map/all_to_all | solution.py:437
  60.2 6.9 %copy-start.1 = (f32[16,2,128]{2,1,0:T(2,128)}, f32[16,2,128]{2,1,0:T(2,128)S(1)}, u32[]{:S(2)}) copy-start(f32[16,2,128]{2,1,0:T(2,128)S(1)} %all-to-all-done.own) | copy-start | bytes 49156
  60.2 6.2 %collective-permute-start.8 = (f32[16,128]{1,0:T(8,128)S(1)}, f32[16,128]{1,0:T(8,128)S(1)}, u32[]{:S(2)}, u32[]{:S(2)}) collective-permute-start(f32[16,128]{1,0:T(8,128)S(1)} %bitcast.14), channel_id=1, source_target_pairs={{0,16},{16,32},{32,48},{48,64},{64,80},{80,96},{96,112},{112,0},{1... | collective-permute-start | bytes 24584 | tf_op jit(solution)/shard_map/ppermute | solution.py:438
  60.3 6.1 %collective-permute-start.9 = (f32[16,128]{1,0:T(8,128)S(1)}, f32[16,128]{1,0:T(8,128)S(1)}, u32[]{:S(2)}, u32[]{:S(2)}) collective-permute-start(f32[16,128]{1,0:T(8,128)S(1)} %bitcast.13), channel_id=1, source_target_pairs={{0,112},{16,0},{32,16},{48,32},{64,48},{80,64},{96,80},{112,96},{1... | collective-permute-start | bytes 24584 | tf_op jit(solution)/shard_map/ppermute | solution.py:439
  66.4 0.7 copy-start.13
  66.4 0.7 copy-start.14
